TPU v7x, 512 devices: a whole 4x8x8 slice. The times are simulated.
512 devices in a mesh: dp: 8 (over x, y_hi), expert: 64 (over y_lo, z, core).
Axes of the slice: x: 4, y: 8 (y_hi: 2, y_lo: 4; y = y_hi * 4 + y_lo), z: 8, core: 2. Of those that a mesh axis runs over, the one named last changes fastest.
Arguments:
- tokens: bfloat16 [65536, 3584], P(('dp', 'expert')), may hold values from -6 to 6
- out_grad: bfloat16 [65536, 3584], P(('dp', 'expert')), may hold values from -1.1953125 to 1.1953125
- gate_weight: bfloat16 [3584, 32768], P('dp', 'expert'), may hold values from -0.09375 to 0.09375
- up_weight: bfloat16 [3584, 32768], P('dp', 'expert'), may hold values from -0.09375 to 0.09375
- route_ids: int32 [65536, 8], P(('dp', 'expert')), may hold values from 0 to 255, all different within a row; in each aligned block of 128 rows (0 to 127, 128 to 255, ...) at most 6 rows name the same one
- route_weights: float32 [65536, 8], P(('dp', 'expert')), may hold values from 0.02 to 0.5
Outputs:
- grad_down: bfloat16 [32768, 3584], P(('expert', 'dp'))
Inputs may be any that keep to these rules, and one draw needn't show every extreme that they name: `route_ids`: each row names 8 different experts. At most 6 of the rows of one device name any one expert, a bound that some block reaches.
All inputs are finite; a program needn't handle non-finite values.
Results may differ from a plain program's by a relative error of at most 0.015.
Values may be sent and summed in bfloat16 or wider, within the bound.
A program may use at most 128 MiB of HBM per device.

v0:
```python
import jax
import jax.numpy as jnp
from jax import lax
from jax.sharding import PartitionSpec as P

N_ROUTED = 256
LOG_SPLIT = 2


def pack_rows(tokens, out_grad, route_ids, route_weights, experts, row_cap):
    expert_ids = jnp.arange(experts, dtype=jnp.int32)
    matches = route_ids[:, :, None] == expert_ids[None, None, :]
    chosen = jnp.any(matches, axis=1)
    scales = jnp.sum(jnp.where(matches, route_weights[:, :, None], 0.0), axis=1)
    order_rank = jnp.cumsum(chosen.astype(jnp.int32), axis=0) - 1
    slot_ids = jnp.arange(row_cap, dtype=jnp.int32)
    pick_table = chosen.T[:, None, :] & (order_rank.T[:, None, :] == slot_ids[None, :, None])
    pick_flat = pick_table.reshape(experts * row_cap, tokens.shape[0])
    pick_values = pick_flat.astype(jnp.bfloat16)
    sent_rows = jnp.dot(pick_values, tokens, preferred_element_type=jnp.float32).astype(
        jnp.bfloat16
    )
    picked_grads = jnp.dot(pick_values, out_grad, preferred_element_type=jnp.float32)
    slot_scales = jnp.sum(jnp.where(pick_table, scales.T[:, None, :], 0.0), axis=2).reshape(
        experts * row_cap, 1
    )
    scaled = (picked_grads * slot_scales).astype(jnp.bfloat16)
    counts = jnp.sum(chosen.astype(jnp.int32), axis=0)
    return (jnp.stack([sent_rows, scaled]), counts)


def per_device(tokens, out_grad, gate_weight, up_weight, route_ids, route_weights):
    split_count = 2**LOG_SPLIT
    experts = lax.axis_size("expert") // split_count
    feature_count = tokens.shape[1]
    row_cap = max(2, tokens.shape[0] * route_ids.shape[1] * 3 // (2 * N_ROUTED))
    paired, counts = pack_rows(tokens, out_grad, route_ids, route_weights, experts, row_cap)
    spread = jnp.broadcast_to(
        paired.reshape(2, experts, 1, row_cap, feature_count),
        (2, experts, split_count, row_cap, feature_count),
    )
    spread = spread.reshape(2, experts * split_count * row_cap, feature_count)
    received = lax.all_to_all(spread, "expert", split_axis=1, concat_axis=1, tiled=True)
    rows_x = received[0]
    rows_dy = received[1]
    columns = rows_x
    gate_pre = jnp.dot(
        columns,
        lax.all_gather(gate_weight, "dp", axis=0, tiled=True),
        preferred_element_type=jnp.float32,
    )
    up_pre = jnp.dot(
        columns,
        lax.all_gather(up_weight, "dp", axis=0, tiled=True),
        preferred_element_type=jnp.float32,
    )
    hidden = (jax.nn.silu(gate_pre) * up_pre).astype(jnp.bfloat16)
    columns = hidden
    return lax.psum_scatter(
        lax.dot_general(
            columns, rows_dy, (((0,), (0,)), ((), ())), preferred_element_type=jnp.float32
        ).astype(jnp.bfloat16),
        "dp",
        scatter_dimension=0,
        tiled=True,
    )


def solution(mesh):
    return jax.shard_map(
        per_device,
        mesh=mesh,
        in_specs=(
            P(("dp", "expert"), None),
            P(("dp", "expert"), None),
            P("dp", "expert"),
            P("dp", "expert"),
            P(("dp", "expert"), None),
            P(("dp", "expert"), None),
        ),
        out_specs=P(("expert", "dp"), None),
        check_vma=False,
    )
```

profile of v0, /device:TPU:8, one launch (start us, length us, event | category | flops | bytes accessed | tf_op | source)
XLA Modules:
  0.0 417.4 jit_solution(7861766384331546865)
XLA Ops:
  6.5 0.0 copy-start
  6.5 0.8 fusion.18
  7.3 0.1 copy.21
  7.4 0.2 reduce_window_sum.11
  7.6 0.1 copy.22
  7.8 0.1 eq.43
  7.8 0.7 select_reduce_fusion.1
  8.6 0.1 select_reduce_fusion
  8.7 0.1 mul.17
  8.8 0.1 compare_and_fusion
  8.8 0.0 copy-done
  8.9 0.3 fusion
  9.2 0.2 stack.10
  9.4 1.5 convolution_convert_fusion.1
  11.0 0.2 stack.9
  11.2 0.4 maximum_bitcast_fusion
  11.6 1.4 copy.23
  13.1 4.0 broadcast_in_dim.43
  17.1 14.5 %all-to-all-start = ((bf16[2,384,3584]{2,0,1:T(2,128)(2,1)}), bf16[2,384,3584]{2,0,1:T(2,128)(2,1)}, u32[]{:S(2)}, u32[]{:S(2)}) async-start(bf16[2,384,3584]{2,0,1:T(2,128)(2,1)} %bitcast.27), calls=%async_computation | async-start | bytes 11010048 | tf_op jit(solution)/shard_map/all_to_all | solution.py:43
  31.6 0.0 all-gather.3.cloned.1.call-start
  31.6 0.7 all-gather.3.cloned.1.call-update
  32.3 0.0 all-gather.5.cloned.1.call-start
  32.4 0.7 all-gather.5.cloned.1.call-update
  33.1 0.0 reduce-scatter.2.cloned.1.call-start
  33.1 192.5 %all-to-all-done = bf16[2,384,3584]{2,0,1:T(2,128)(2,1)} async-done(((bf16[2,384,3584]{2,0,1:T(2,128)(2,1)}), bf16[2,384,3584]{2,0,1:T(2,128)(2,1)}, u32[]{:S(2)}, u32[]{:S(2)}) %all-to-all-start) | async-done | bytes 5505056 | tf_op jit(solution)/shard_map/all_to_all | solution.py:43
  225.7 14.0 %fusion.21 = (bf16[1,384,3584]{2,0,1:T(2,128)(2,1)}, bf16[1,384,3584]{2,0,1:T(2,128)(2,1)}) fusion(bf16[2,384,3584]{2,0,1:T(2,128)(2,1)} %all-to-all-done), kind=kLoop, calls=%fused_computation.25 | loop fusion | bytes 11010048 | tf_op jit(solution)/shard_map/slice | solution.py:44
  239.7 0.0 all-gather.3.cloned.1.call-done
  239.7 5.2 %fusion.5 = f32[384,512]{1,0:T(8,128)S(1)} fusion(bf16[3584,512]{1,0:T(8,128)(2,1)} %all-gather.3.cloned.1.call-done, bf16[1,384,3584]{2,0,1:T(2,128)(2,1)} %get-tuple-element.5), kind=kOutput, calls=%fused_computation.8 | convolution fusion | flops 1409286144 | bytes 7208960 | tf_op jit(solution)/shard_map/dot_general | solution.py:47
  245.0 41.1 %all-gather.5.cloned.1.call-done = bf16[3584,512]{1,0:T(8,128)(2,1)} async-done(((bf16[448,512]{1,0:T(8,128)(2,1)}), bf16[3584,512]{1,0:T(8,128)(2,1)}) %all-gather.5.cloned.1.call-update) | async-done | bytes 3670032 | tf_op jit(solution)/shard_map/all_gather | solution.py:54
  286.1 10.7 %convolution_convert_fusion = bf16[512,3584]{1,0:T(8,128)(2,1)} fusion(bf16[1,384,3584]{2,0,1:T(2,128)(2,1)} %get-tuple-element.6, bf16[3584,512]{1,0:T(8,128)(2,1)} %all-gather.5.cloned.1.call-done, bf16[1,384,3584]{2,0,1:T(2,128)(2,1)} %get-tuple-element.5, f32[384,512]{1,0:T(8,128)S(1)} %fusion.5), kind=kOutput, calls=%fused_computation | convolution fusion | flops 2821586944 | bytes 13631488 | tf_op jit(solution)/shard_map/dot_general | solution.py:60
  296.8 0.0 reduce-scatter.2.cloned.1.call-update
  296.8 114.0 %reduce-scatter.2.cloned.1.call-done = bf16[64,3584]{1,0:T(8,128)(2,1)} async-done(((bf16[512,3584]{1,0:T(8,128)(2,1)}), bf16[64,3584]{1,0:T(8,128)(2,1)}) %reduce-scatter.2.cloned.1.call-update) | async-done | bytes 458768 | tf_op jit(solution)/shard_map/reduce_scatter | solution.py:59
  (7 shorter events, 0.1 us)
Async XLA Ops:
  6.5 2.3 copy-start
  17.1 208.6 %all-to-all-start = ((bf16[2,384,3584]{2,0,1:T(2,128)(2,1)}), bf16[2,384,3584]{2,0,1:T(2,128)(2,1)}, u32[]{:S(2)}, u32[]{:S(2)}) async-start(bf16[2,384,3584]{2,0,1:T(2,128)(2,1)} %bitcast.27), calls=%async_computation | async-start | bytes 11010048 | tf_op jit(solution)/shard_map/all_to_all | solution.py:43
  31.6 208.1 %all-gather.3.cloned.1.call-start = ((), (), s32[]{:S(2)}) async-start(), calls=%async_computation.2 | async-start | bytes 4128768 | tf_op jit(solution)/shard_map/all_gather | solution.py:49
  32.3 253.8 %all-gather.5.cloned.1.call-start = ((), (), s32[]{:S(2)}) async-start(), calls=%async_computation.3 | async-start | bytes 4128768 | tf_op jit(solution)/shard_map/all_gather | solution.py:54
  33.1 377.7 %reduce-scatter.2.cloned.1.call-start = ((), (), s32[]{:S(2)}) async-start(), calls=%async_computation.4 | async-start | bytes 4128768 | tf_op jit(solution)/shard_map/reduce_scatter | solution.py:59
Sparse Core Ops, SparseCore 0:
  35.6 143.5 all-gather.2
  182.4 103.6 all-gather.4
  297.0 113.8 reduce-scatter.1
where the time goes:
time: 418 us; the launch traced here: 417 us
  waiting for transfers between devices  349 us (83%)
  local copies, waits for them, and re-layouts  20.3 us (5%)
  matrix products  17.8 us (4%)
  starting transfers between devices  14.6 us (3%)
  between operations  13.2 us (3%)
    all_to_all x1, waiting for transfers between devices, per_device(): lax.all_to_all(spread, 'expert', split_axis=1, concat_axis=1, tiled=True)  193 us
    reduce_scatter x1, waiting for transfers between devices, per_device(): lax.psum_scatter(lax.dot_general(columns, rows_dy, (((0,), (0,)), ((), ()...  114 us
    all_gather x1, waiting for transfers between devices, per_device(): lax.all_gather(up_weight, 'dp', axis=0, tiled=True)  41.1 us
    all_to_all x1, starting transfers between devices, per_device(): lax.all_to_all(spread, 'expert', split_axis=1, concat_axis=1, tiled=True)  14.5 us
    slice x1, local copies, waits for them, and re-layouts, per_device(): rows_x = received[0]  14 us
    dot_general x1, matrix products, per_device(): lax.dot_general(columns, rows_dy, (((0,), (0,)), ((), ())), preferred_ele...  10.7 us
  transfers between devices with their start and end apart: 4, of which 3 were waited for; matrix products, arithmetic and copies ran while one was open for 5% of the time, Pallas kernels for 0%

commit v1 on v0

--- a/solution.py
+++ b/solution.py
@@ -51,7 +51,9 @@
     )
     up_pre = jnp.dot(
         columns,
-        lax.all_gather(up_weight, "dp", axis=0, tiled=True),
+        jnp.concatenate(
+            lax.all_to_all(jnp.stack([up_weight] * lax.axis_size("dp")), "dp", 0, 0), axis=0
+        ),
         preferred_element_type=jnp.float32,
     )
     hidden = (jax.nn.silu(gate_pre) * up_pre).astype(jnp.bfloat16)

time: 418 us -> 484 us (1.16)
  waiting for transfers between devices: 349 us -> 405 us
  starting transfers between devices: 14.6 us -> 22.2 us
    reduce_scatter x1, waiting for transfers between devices: 114 us -> 172 us  [per_device(): lax.psum_scatter(lax.dot_general(columns, rows_dy, (((0,), (0,)), ((), ()...]
    all_to_all x0 -> x1, waiting for transfers between devices: none -> 50.1 us  [per_device(): lax.all_to_all(jnp.stack([up_weight] * lax.axis_size('dp')), 'dp', 0, 0)]
    all_gather x1 -> x0, waiting for transfers between devices: 41.1 us -> none  [per_device(): lax.all_gather(up_weight, 'dp', axis=0, tiled=True)]
    all_to_all x1, waiting for transfers between devices: 193 us -> 183 us  [per_device(): lax.all_to_all(spread, 'expert', split_axis=1, concat_axis=1, tiled=True)]
    all_to_all x0 -> x1, starting transfers between devices: none -> 7.43 us  [per_device(): lax.all_to_all(jnp.stack([up_weight] * lax.axis_size('dp')), 'dp', 0, 0)]
  transfers between devices with their start and end apart: 4 -> 4, of which waited for: 3 -> 3; matrix products, arithmetic and copies ran while one was open for 5% -> 4% of each run, Pallas kernels for 0% -> 0%
where the time goes in v1:
time: 484 us
  waiting for transfers between devices  405 us (84%)
  local copies, waits for them, and re-layouts  22.5 us (5%)
  starting transfers between devices  22.2 us (5%)
  matrix products  17.8 us (4%)
  between operations  13.5 us (3%)
    all_to_all x1, waiting for transfers between devices, per_device(): lax.all_to_all(spread, 'expert', split_axis=1, concat_axis=1, tiled=True)  183 us
    reduce_scatter x1, waiting for transfers between devices, per_device(): lax.psum_scatter(lax.dot_general(columns, rows_dy, (((0,), (0,)), ((), ()...  172 us
    all_to_all x1, waiting for transfers between devices, per_device(): lax.all_to_all(jnp.stack([up_weight] * lax.axis_size('dp')), 'dp', 0, 0)  50.1 us
    all_to_all x1, starting transfers between devices, per_device(): lax.all_to_all(spread, 'expert', split_axis=1, concat_axis=1, tiled=True)  14.7 us
    slice x1, local copies, waits for them, and re-layouts, per_device(): rows_x = received[0]  14 us
    dot_general x1, matrix products, per_device(): lax.dot_general(columns, rows_dy, (((0,), (0,)), ((), ())), preferred_ele...  10.7 us
  transfers between devices with their start and end apart: 4, of which 3 were waited for; matrix products, arithmetic and copies ran while one was open for 4% of the time, Pallas kernels for 0%

profile of v1, /device:TPU:8, one launch (start us, length us, event | category | flops | bytes accessed | tf_op | source)
XLA Modules:
  0.0 483.7 jit_solution(17962650513037921193)
XLA Ops:
  6.5 0.0 copy-start
  6.5 0.8 fusion.18
  7.4 0.1 copy.21
  7.5 0.2 reduce_window_sum.11
  7.7 0.1 copy.22
  7.8 0.1 eq.43
  7.8 0.7 select_reduce_fusion.1
  8.6 0.1 select_reduce_fusion
  8.7 0.1 mul.17
  8.8 0.1 compare_and_fusion
  8.8 0.0 copy-done
  8.9 0.3 fusion
  9.2 0.2 stack.9
  9.4 1.5 convolution_convert_fusion.1
  11.0 0.2 stack.8
  11.2 0.4 maximum_bitcast_fusion
  11.6 1.4 copy.23
  13.1 4.0 broadcast_in_dim.43
  17.1 0.0 copy-start.1
  17.1 14.7 %all-to-all-start = ((bf16[2,384,3584]{2,0,1:T(2,128)(2,1)}), bf16[2,384,3584]{2,0,1:T(2,128)(2,1)}, u32[]{:S(2)}, u32[]{:S(2)}) async-start(bf16[2,384,3584]{2,0,1:T(2,128)(2,1)} %bitcast.28), calls=%async_computation | async-start | bytes 11010048 | tf_op jit(solution)/shard_map/all_to_all | solution.py:43
  31.7 0.0 all-gather.2.cloned.1.call-start
  31.8 0.7 all-gather.2.cloned.1.call-update
  32.5 182.9 %all-to-all-done = bf16[2,384,3584]{2,0,1:T(2,128)(2,1)} async-done(((bf16[2,384,3584]{2,0,1:T(2,128)(2,1)}), bf16[2,384,3584]{2,0,1:T(2,128)(2,1)}, u32[]{:S(2)}, u32[]{:S(2)}) %all-to-all-start) | async-done | bytes 5505056 | tf_op jit(solution)/shard_map/all_to_all | solution.py:43
  215.4 0.0 copy-done.1
  215.4 2.2 stack.11
  217.6 7.4 %all-to-all-start.1 = ((bf16[8,448,512]{2,1,0:T(8,128)(2,1)}), bf16[8,448,512]{2,1,0:T(8,128)(2,1)}, u32[]{:S(2)}, u32[]{:S(2)}) async-start(bf16[8,448,512]{2,1,0:T(8,128)(2,1)} %stack.11), calls=%async_computation.1 | async-start | bytes 7340032 | tf_op jit(solution)/shard_map/all_to_all | solution.py:55
  225.0 0.0 reduce-scatter.2.cloned.1.call-start
  225.0 14.0 %fusion.21 = (bf16[1,384,3584]{2,0,1:T(2,128)(2,1)}, bf16[1,384,3584]{2,0,1:T(2,128)(2,1)}) fusion(bf16[2,384,3584]{2,0,1:T(2,128)(2,1)} %all-to-all-done), kind=kLoop, calls=%fused_computation.25 | loop fusion | bytes 11010048 | tf_op jit(solution)/shard_map/slice | solution.py:44
  239.1 0.0 all-gather.2.cloned.1.call-done
  239.1 5.2 %fusion.5 = f32[384,512]{1,0:T(8,128)S(1)} fusion(bf16[3584,512]{1,0:T(8,128)(2,1)} %all-gather.2.cloned.1.call-done, bf16[1,384,3584]{2,0,1:T(2,128)(2,1)} %get-tuple-element.5), kind=kOutput, calls=%fused_computation.8 | convolution fusion | flops 1409286144 | bytes 7208960 | tf_op jit(solution)/shard_map/dot_general | solution.py:47
  244.3 50.1 %all-to-all-done.1 = bf16[8,448,512]{2,1,0:T(8,128)(2,1)} async-done(((bf16[8,448,512]{2,1,0:T(8,128)(2,1)}), bf16[8,448,512]{2,1,0:T(8,128)(2,1)}, u32[]{:S(2)}, u32[]{:S(2)}) %all-to-all-start.1) | async-done | bytes 3670048 | tf_op jit(solution)/shard_map/all_to_all | solution.py:55
  294.4 10.7 %convolution_convert_fusion = bf16[512,3584]{1,0:T(8,128)(2,1)} fusion(bf16[1,384,3584]{2,0,1:T(2,128)(2,1)} %get-tuple-element.6, bf16[3584,512]{1,0:T(8,128)(2,1)} %bitcast.5, bf16[1,384,3584]{2,0,1:T(2,128)(2,1)} %get-tuple-element.5, f32[384,512]{1,0:T(8,128)S(1)} %fusion.5), kind=kOutput, calls=%fused_computation | convolution fusion | flops 2821586944 | bytes 13631488 | tf_op jit(solution)/shard_map/dot_general | solution.py:62
  305.1 0.0 reduce-scatter.2.cloned.1.call-update
  305.2 171.7 %reduce-scatter.2.cloned.1.call-done = bf16[64,3584]{1,0:T(8,128)(2,1)} async-done(((bf16[512,3584]{1,0:T(8,128)(2,1)}), bf16[64,3584]{1,0:T(8,128)(2,1)}) %reduce-scatter.2.cloned.1.call-update) | async-done | bytes 458768 | tf_op jit(solution)/shard_map/reduce_scatter | solution.py:61
  (7 shorter events, 0.1 us)
Async XLA Ops:
  6.5 2.3 copy-start
  17.1 198.3 %copy-start.1 = (bf16[448,512]{1,0:T(8,128)(2,1)S(1)}, bf16[448,512]{1,0:T(8,128)(2,1)}, u32[]{:S(2)}) copy-start(bf16[448,512]{1,0:T(8,128)(2,1)} %param.9) | copy-start | bytes 1376260
  17.1 198.3 %all-to-all-start = ((bf16[2,384,3584]{2,0,1:T(2,128)(2,1)}), bf16[2,384,3584]{2,0,1:T(2,128)(2,1)}, u32[]{:S(2)}, u32[]{:S(2)}) async-start(bf16[2,384,3584]{2,0,1:T(2,128)(2,1)} %bitcast.28), calls=%async_computation | async-start | bytes 11010048 | tf_op jit(solution)/shard_map/all_to_all | solution.py:43
  31.7 207.3 %all-gather.2.cloned.1.call-start = ((), (), s32[]{:S(2)}) async-start(), calls=%async_computation.3 | async-start | bytes 4128768 | tf_op jit(solution)/shard_map/all_gather | solution.py:49
  217.6 76.9 %all-to-all-start.1 = ((bf16[8,448,512]{2,1,0:T(8,128)(2,1)}), bf16[8,448,512]{2,1,0:T(8,128)(2,1)}, u32[]{:S(2)}, u32[]{:S(2)}) async-start(bf16[8,448,512]{2,1,0:T(8,128)(2,1)} %stack.11), calls=%async_computation.1 | async-start | bytes 7340032 | tf_op jit(solution)/shard_map/all_to_all | solution.py:55
  225.0 251.9 %reduce-scatter.2.cloned.1.call-start = ((), (), s32[]{:S(2)}) async-start(), calls=%async_computation.4 | async-start | bytes 4128768 | tf_op jit(solution)/shard_map/reduce_scatter | solution.py:61
Sparse Core Ops, SparseCore 0:
  35.8 143.3 all-gather.1
  305.3 171.5 reduce-scatter.1
